TPU v7x, 32 devices: a whole 2x2x4 slice. The times are simulated.
32 devices in a mesh: pair: 8 (over z, x), row: 4 (over y, core).
Axes of the slice: x: 2, y: 2, z: 4, core: 2. Of those that a mesh axis runs over, the one named last changes fastest.
Arguments:
- records: bfloat16 [128, 4096, 8], P('row', 'pair'), may hold values from -10 to 10
- offsets: float32 [8, 128], P('pair', 'row'), may hold values from -1 to 1
- counts: int32 [8], replicated, may hold values from 64 to 128, as said below
- damping: float32 [1], replicated, may hold values from 0.1 to 1
Outputs:
- offset_step: float32 [8, 128], P('pair', 'row')
Inputs may be any that keep to these rules, and one draw needn't show every extreme that they name: Channel i of block b is live when i < counts[b]; in every draw some block has all 128 channels live.
All inputs are finite; a program needn't handle non-finite values.
Results may differ from a plain program's by a relative error of at most 0.0044.
Values may be sent and summed in bfloat16 or wider, within the bound.
No kernel may reach another device: no remote copies, remote signals or barrier semaphores. Data moves between devices by JAX's collectives and lax.ppermute only.
A program may use at most 64 MiB of HBM per device.

v0:
```python
import math
import jax
import jax.numpy as jnp
from jax import lax
from jax.sharding import PartitionSpec as P

CB = 128
NF = 512
NLAG = 256


def band_table(row_start, row_count, samples, first_bin, freq_count):
    sample_ids = row_start + jnp.arange(row_count, dtype=jnp.int32)
    freq_bins = first_bin + jnp.arange(freq_count, dtype=jnp.int32)
    phase_ids = sample_ids[:, None] * freq_bins[None, :] % samples
    angles = phase_ids.astype(jnp.float32) * (2.0 * math.pi / samples)
    return jnp.concatenate([jnp.cos(angles), jnp.sin(angles)], axis=1)


def lag_weights(samples, first_bin, freq_count, lag_count):
    freq_bins = first_bin + jnp.arange(freq_count, dtype=jnp.int32)
    lag_ids = 1 + jnp.arange(lag_count, dtype=jnp.int32)
    phase_ids = freq_bins[:, None] * lag_ids[None, :] % samples
    angles = phase_ids.astype(jnp.float32) * (2.0 * math.pi / samples)
    centre = (jnp.arange(freq_count, dtype=jnp.float32) + 0.5) * (math.pi / freq_count)
    weight = jnp.sin(centre) ** 2
    return (-2.0 * weight[:, None] * jnp.sin(angles)).astype(jnp.bfloat16)


def pair_stats(own_spec, partners, lag_table, angular):
    own_re = own_spec[:, 0].astype(jnp.float32)
    own_im = own_spec[:, 1].astype(jnp.float32)
    far_re = partners[:, :, 0].astype(jnp.float32)
    far_im = partners[:, :, 1].astype(jnp.float32)
    cross_re = own_re * far_re + own_im * far_im
    cross_im = own_im * far_re - own_re * far_im
    stacked = jnp.stack([cross_im, angular * cross_re]).astype(jnp.bfloat16)
    lagged = jnp.dot(stacked, lag_table, preferred_element_type=jnp.float32)
    residual = lagged[0]
    jacobian = lagged[1]
    return (jnp.sum(jacobian * jacobian, axis=-1), jnp.sum(jacobian * residual, axis=-1))


def per_device(records, offsets, counts, damping):
    nblock = lax.axis_size("pair")
    block_rank = lax.axis_index("pair")
    quarter = lax.axis_index("row")
    relaid = lax.all_to_all(records, "pair", split_axis=2, concat_axis=1, tiled=True)
    signal = relaid[:, :, 0]
    channels = signal.shape[0]
    samples = signal.shape[1]
    first_bin = samples // 8
    block_len = samples // 8

    def accumulate(partial_value, turn_index):
        first_row = turn_index * block_len
        segment = lax.dynamic_slice_in_dim(signal, first_row, block_len, 1)
        dft_table = band_table(first_row, block_len, samples, first_bin, NF)
        table_high = dft_table.astype(jnp.bfloat16)
        table_low = (dft_table - table_high.astype(jnp.float32)).astype(jnp.bfloat16)
        partial_value = partial_value + jnp.dot(
            segment, table_high, preferred_element_type=jnp.float32
        )
        partial_value = partial_value + jnp.dot(
            segment, table_low, preferred_element_type=jnp.float32
        )
        return (partial_value, None)

    spectrum, _ = lax.scan(
        accumulate, jnp.zeros((channels, 2 * NF), jnp.float32), jnp.arange(8, dtype=jnp.int32)
    )
    cosine_part = spectrum[:, :NF]
    sine_part = spectrum[:, NF:]
    angular = (first_bin + jnp.arange(NF, dtype=jnp.int32)).astype(jnp.float32) * (
        2.0 * math.pi / samples
    )
    shift_angle = offsets[0][:, None] * angular[None, :]
    shift_cos = jnp.cos(shift_angle)
    shift_sin = jnp.sin(shift_angle)
    real_part = cosine_part * shift_cos + sine_part * shift_sin
    imag_part = cosine_part * shift_sin - sine_part * shift_cos
    live_count = lax.dynamic_index_in_dim(counts, block_rank, keepdims=False)
    channel_ids = quarter * channels + jnp.arange(channels, dtype=jnp.int32)
    alive = (channel_ids < live_count).astype(jnp.float32)
    energy = jnp.mean(real_part * real_part + imag_part * imag_part, axis=1)
    weight_scale = alive / jnp.sqrt(energy + 1e-06)
    own_spec = jnp.stack(
        [real_part * weight_scale[:, None], imag_part * weight_scale[:, None]], axis=1
    ).astype(jnp.bfloat16)
    lag_table = lag_weights(samples, first_bin, NF, NLAG)
    segment = lax.all_gather(own_spec[None], "pair", axis=0, tiled=True)
    squares_part, products_part = pair_stats(own_spec, segment, lag_table, angular)
    partner_ids = jnp.arange(segment.shape[0], dtype=jnp.int32)
    keep_mask = (partner_ids > block_rank).astype(jnp.float32)[:, None]
    new_squares = squares_part * keep_mask
    new_products = products_part * keep_mask
    eye_blocks = jnp.eye(nblock, dtype=jnp.float32)
    onehot = (jnp.arange(nblock, dtype=jnp.int32) == block_rank).astype(jnp.float32)
    sq_t = new_squares.T
    pr_t = new_products.T
    crossing = sq_t[:, None, :] * onehot[None, :, None]
    diag_vals = sq_t + onehot[None, :] * jnp.sum(sq_t, axis=1, keepdims=True)
    hessian = diag_vals[:, :, None] * eye_blocks[None] - crossing - jnp.swapaxes(crossing, 1, 2)
    gradient = onehot[None, :] * jnp.sum(pr_t, axis=1, keepdims=True) - pr_t
    hessian, gradient = lax.psum((hessian, gradient), "pair")
    diagonal = jnp.diagonal(hessian, axis1=1, axis2=2)
    trace_sum = lax.psum(jnp.sum(diagonal), "row")
    level_mean = trace_sum / (nblock * CB)
    damped = damping[0] * (diagonal + level_mean)
    system = hessian + damped[:, :, None] * eye_blocks[None]
    factor = jnp.linalg.cholesky(system)
    update = -jax.scipy.linalg.cho_solve((factor, True), gradient[:, :, None])[:, :, 0]
    return lax.dynamic_slice_in_dim(update, block_rank, 1, 1).T


def solution(mesh):
    return jax.shard_map(
        per_device,
        mesh=mesh,
        in_specs=(P("row", "pair", None), P("pair", "row"), P(), P()),
        out_specs=P("pair", "row"),
        check_vma=False,
    )
```

profile of v0, /device:TPU:0, one launch (start us, length us, event | category | flops | bytes accessed | tf_op | source)
XLA Modules:
  0.0 172.0 jit_solution(3710374380044799579)
XLA Ops:
  0.0 1.7 %copy.35 = bf16[32,512,8]{1,0,2:T(8,128)(2,1)} copy(bf16[32,512,8]{1,2,0:T(8,128)(2,1)} %param.6) | data formatting | bytes 524288 | tf_op args[0]
  1.7 7.3 %all-to-all-start = ((bf16[32,512,8]{1,0,2:T(8,128)(2,1)}), bf16[32,512,8]{1,0,2:T(8,128)(2,1)S(1)}, u32[]{:S(2)}, u32[]{:S(2)}) async-start(bf16[32,512,8]{1,0,2:T(8,128)(2,1)} %copy.35), calls=%async_computation | async-start | bytes 524288 | tf_op jit(solution)/shard_map/all_to_all | solution.py:48
  9.2 0.6 dynamic_slice.20
  9.9 8.1 %all-to-all-done = bf16[32,512,8]{1,0,2:T(8,128)(2,1)S(1)} async-done(((bf16[32,512,8]{1,0,2:T(8,128)(2,1)}), bf16[32,512,8]{1,0,2:T(8,128)(2,1)S(1)}, u32[]{:S(2)}, u32[]{:S(2)}) %all-to-all-start) | async-done | bytes 262176 | tf_op jit(solution)/shard_map/all_to_all | solution.py:48
  18.0 48.9 %while.13 = (s32[]{:T(128)}, f32[32,1024]{1,0:T(8,128)S(1)}, s32[8]{0:T(128)S(1)}, bf16[32,4096]{1,0:T(8,128)(2,1)S(1)}, s32[]{:T(128)}, /*index=5*/s32[1]{0:T(128)}, s32[]{:T(128)}, s32[]{:T(128)}) while((s32[]{:T(128)}, f32[32,1024]{1,0:T(8,128)S(1)}, s32[8]{0:T(128)S(1)}, bf16[32,4096]{1,0:T(8,128)(2,1)S(1)}, s32[]{:T(128)}, ...), condition=%wide.region_1.2_spmd.clone, body=%wide.region_0.1_spmd.clone.sunk | while | flops 75596808 | bytes 6889645 | solution.py:69
  18.0 0.7 dynamic_slice.34
  19.4 4.1 %fusion.70 = (f32[512,512]{1,0:T(8,128)S(1)}, f32[512,512]{1,0:T(8,128)S(1)}) fusion(s32[512]{0:T(512)S(1)} %get-tuple-element.138, s32[512]{0:T(512)S(1)} %get-tuple-element.139), kind=kLoop, calls=%fused_computation.16.clone.1 | loop fusion | flops 3670016 | bytes 2101248 | tf_op jit(solution)/shard_map/while/body/eval_jaxpr/cos | solution.py:17
  23.5 0.3 fusion.71
  23.8 0.3 convolution_add_fusion.2
  24.1 0.7 dynamic_slice.34
  25.5 4.1 %fusion.70 = (f32[512,512]{1,0:T(8,128)S(1)}, f32[512,512]{1,0:T(8,128)S(1)}) fusion(s32[512]{0:T(512)S(1)} %get-tuple-element.138, s32[512]{0:T(512)S(1)} %get-tuple-element.139), kind=kLoop, calls=%fused_computation.16.clone.1 | loop fusion | flops 3670016 | bytes 2101248 | tf_op jit(solution)/shard_map/while/body/eval_jaxpr/cos | solution.py:17
  29.6 0.3 fusion.71
  29.9 0.3 convolution_add_fusion.2
  30.2 0.7 dynamic_slice.34
  31.6 4.1 %fusion.70 = (f32[512,512]{1,0:T(8,128)S(1)}, f32[512,512]{1,0:T(8,128)S(1)}) fusion(s32[512]{0:T(512)S(1)} %get-tuple-element.138, s32[512]{0:T(512)S(1)} %get-tuple-element.139), kind=kLoop, calls=%fused_computation.16.clone.1 | loop fusion | flops 3670016 | bytes 2101248 | tf_op jit(solution)/shard_map/while/body/eval_jaxpr/cos | solution.py:17
  35.8 0.3 fusion.71
  36.1 0.3 convolution_add_fusion.2
  36.3 0.7 dynamic_slice.34
  37.7 4.1 %fusion.70 = (f32[512,512]{1,0:T(8,128)S(1)}, f32[512,512]{1,0:T(8,128)S(1)}) fusion(s32[512]{0:T(512)S(1)} %get-tuple-element.138, s32[512]{0:T(512)S(1)} %get-tuple-element.139), kind=kLoop, calls=%fused_computation.16.clone.1 | loop fusion | flops 3670016 | bytes 2101248 | tf_op jit(solution)/shard_map/while/body/eval_jaxpr/cos | solution.py:17
  41.9 0.3 fusion.71
  42.2 0.3 convolution_add_fusion.2
  42.5 0.7 dynamic_slice.34
  43.8 4.1 %fusion.70 = (f32[512,512]{1,0:T(8,128)S(1)}, f32[512,512]{1,0:T(8,128)S(1)}) fusion(s32[512]{0:T(512)S(1)} %get-tuple-element.138, s32[512]{0:T(512)S(1)} %get-tuple-element.139), kind=kLoop, calls=%fused_computation.16.clone.1 | loop fusion | flops 3670016 | bytes 2101248 | tf_op jit(solution)/shard_map/while/body/eval_jaxpr/cos | solution.py:17
  48.0 0.3 fusion.71
  48.3 0.3 convolution_add_fusion.2
  48.6 0.7 dynamic_slice.34
  50.0 4.1 %fusion.70 = (f32[512,512]{1,0:T(8,128)S(1)}, f32[512,512]{1,0:T(8,128)S(1)}) fusion(s32[512]{0:T(512)S(1)} %get-tuple-element.138, s32[512]{0:T(512)S(1)} %get-tuple-element.139), kind=kLoop, calls=%fused_computation.16.clone.1 | loop fusion | flops 3670016 | bytes 2101248 | tf_op jit(solution)/shard_map/while/body/eval_jaxpr/cos | solution.py:17
  54.1 0.3 fusion.71
  54.4 0.3 convolution_add_fusion.2
  54.7 0.7 dynamic_slice.34
  56.1 4.1 %fusion.70 = (f32[512,512]{1,0:T(8,128)S(1)}, f32[512,512]{1,0:T(8,128)S(1)}) fusion(s32[512]{0:T(512)S(1)} %get-tuple-element.138, s32[512]{0:T(512)S(1)} %get-tuple-element.139), kind=kLoop, calls=%fused_computation.16.clone.1 | loop fusion | flops 3670016 | bytes 2101248 | tf_op jit(solution)/shard_map/while/body/eval_jaxpr/cos | solution.py:17
  60.2 0.3 fusion.71
  60.5 0.3 convolution_add_fusion.2
  60.8 0.7 dynamic_slice.34
  62.2 4.1 %fusion.70 = (f32[512,512]{1,0:T(8,128)S(1)}, f32[512,512]{1,0:T(8,128)S(1)}) fusion(s32[512]{0:T(512)S(1)} %get-tuple-element.138, s32[512]{0:T(512)S(1)} %get-tuple-element.139), kind=kLoop, calls=%fused_computation.16.clone.1 | loop fusion | flops 3670016 | bytes 2101248 | tf_op jit(solution)/shard_map/while/body/eval_jaxpr/cos | solution.py:17
  66.4 0.3 fusion.71
  66.6 0.3 convolution_add_fusion.2
  66.9 0.4 add_reduce_fusion
  67.4 0.6 compare_select_fusion
  68.1 31.6 %all_gather.3 = bf16[8,32,2,512]{3,1,0,2:T(8,128)(2,1)S(1)} all-gather(bf16[1,32,2,512]{3,1,0,2:T(8,128)(2,1)S(1)} %pad_maximum_fusion.1), channel_id=1, replica_groups=mesh['pair'=8,'row'=4] {'pair'}, dimensions={0}, use_global_device_ids=true | all-gather | bytes 589824 | tf_op jit(solution)/shard_map/all_gather | solution.py:91
  99.9 2.3 %fusion.28 = f32[2,8,32,256]{3,2,1,0:T(8,128)S(1)} fusion(bf16[1,8,32,512]{3,2,1,0:T(8,128)(2,1)S(1)} %get-tuple-element.99, bf16[1,8,32,512]{3,2,1,0:T(8,128)(2,1)S(1)} %get-tuple-element.98, s32[256]{0:T(256)S(1)} %iota_add_fusion.3, s32[512]{0:T(512)S(1)} %iota_add_fusion.2, f32[512]{0:T(512)S(1)} %multiply_multiply_fusion), kind=kOutput, calls=%fused_computation.45 | convolution fusion | flops 136577024 | bytes 1053696 | tf_op jit(solution)/shard_map/dot_general | solution.py:38
  102.6 35.2 %all-reduce = (f32[32,8,8]{0,1,2:T(8,128)S(1)}, f32[32,8]{0,1:T(8,128)S(1)}) all-reduce(f32[32,8,8]{0,1,2:T(8,128)S(1)} %multiply_subtract_fusion, f32[32,8]{0,1:T(8,128)S(1)} %get-tuple-element.104), channel_id=1, replica_groups=mesh['pair'=8,'row'=4] {'pair'}, use_global_device_ids=true, to_apply=%region_5.6 | all-reduce | flops 2304 | bytes 18432 | tf_op jit(solution)/shard_map/psum | solution.py:105
  137.8 0.6 gather_fusion
  138.4 0.7 reduce_sum.57
  139.7 6.3 %psum.22 = f32[]{:T(128)} all-reduce(f32[]{:T(128)} %reduce_sum.57), channel_id=1, replica_groups=mesh['pair'=8,'row'=4] {'row'}, use_global_device_ids=true, to_apply=%region_7.8 | all-reduce | flops 1 | bytes 8 | tf_op jit(solution)/shard_map/psum | solution.py:107
  146.9 23.5 %custom-call.11 = f32[32,8,8]{2,1,0:T(8,128)S(1)} custom-call(f32[32,8,8]{2,1,0:T(8,128)S(1)} %broadcast_multiply_fusion), custom_call_target="Cholesky" | custom-call | tf_op jit(solution)/shard_map/jit(cholesky)/cholesky | solution.py:111
  170.7 0.7 custom-call.12
  171.5 0.5 dynamic-slice_bitcast_fusion
  (45 shorter events, 1.5 us)
Async XLA Ops:
  0.0 9.2 %copy-start.1 = (s32[8]{0:T(128)S(1)}, s32[8]{0:T(128)}, u32[]{:S(2)}) copy-start(s32[8]{0:T(128)} %param.8) | copy-start | bytes 100
  1.7 16.2 %all-to-all-start = ((bf16[32,512,8]{1,0,2:T(8,128)(2,1)}), bf16[32,512,8]{1,0,2:T(8,128)(2,1)S(1)}, u32[]{:S(2)}, u32[]{:S(2)}) async-start(bf16[32,512,8]{1,0,2:T(8,128)(2,1)} %copy.35), calls=%async_computation | async-start | bytes 524288 | tf_op jit(solution)/shard_map/all_to_all | solution.py:48
  18.0 49.0 %copy-start = (f32[1,32]{1,0:T(1,128)S(1)}, f32[1,32]{1,0:T(1,128)}, u32[]{:S(2)}) copy-start(f32[1,32]{1,0:T(1,128)} %param.7) | copy-start | bytes 388
where the time goes:
time: 172 us
  blocking collectives  73.1 us (42%)
  other arithmetic  60.2 us (35%)
  local copies, waits for them, and re-layouts  9.21 us (5%)
  waiting for transfers between devices  8.06 us (5%)
  starting transfers between devices  7.28 us (4%)
  matrix products  6.83 us (4%)
  loops' own time  5.79 us (3%)
    psum x1, blocking collectives, per_device(): hessian, gradient = lax.psum((hessian, gradient), 'pair')  35.2 us
    cos x8, other arithmetic, band_table(): return jnp.concatenate([jnp.cos(angles), jnp.sin(angles)], axis=1)  33.2 us
    all_gather x1, blocking collectives, per_device(): segment = lax.all_gather(own_spec[None], 'pair', axis=0, tiled=True)  31.6 us
    another operation x4, other arithmetic, per_device(): factor = jnp.linalg.cholesky(system)  23.6 us
    all_to_all x1, waiting for transfers between devices, per_device(): lax.all_to_all(records, 'pair', split_axis=2, concat_axis=1, tiled=True)  8.06 us
    all_to_all x1, starting transfers between devices, per_device(): lax.all_to_all(records, 'pair', split_axis=2, concat_axis=1, tiled=True)  7.28 us
    psum x1, blocking collectives, per_device(): trace_sum = lax.psum(jnp.sum(diagonal), 'row')  6.25 us
    another operation x1, loops' own time, per_device(): lax.scan(accumulate, jnp.zeros((channels, 2 * NF), jnp.float32), jnp.aran...  5.79 us
  transfers between devices with their start and end apart: 1, of which 1 were waited for; matrix products, arithmetic and copies ran while one was open for 0% of the time, Pallas kernels for 0%

commit v1 on v0

--- a/solution.py
+++ b/solution.py
@@ -3,10 +3,18 @@
 import jax.numpy as jnp
 from jax import lax
 from jax.sharding import PartitionSpec as P
+from jax.lax import all_to_all, axis_size
 
 CB = 128
 NF = 512
 NLAG = 256
+
+
+def _pass_task(s0):
+    n_shards = axis_size("pair")
+    lanes = list(map(lambda num: n_shards if num == 0 else 1, range(s0.ndim)))
+    front = all_to_all(jnp.tile(s0, lanes), "pair", split_axis=0, concat_axis=0, tiled=True)
+    return front
 
 
 def band_table(row_start, row_count, samples, first_bin, freq_count):
@@ -88,7 +96,7 @@
         [real_part * weight_scale[:, None], imag_part * weight_scale[:, None]], axis=1
     ).astype(jnp.bfloat16)
     lag_table = lag_weights(samples, first_bin, NF, NLAG)
-    segment = lax.all_gather(own_spec[None], "pair", axis=0, tiled=True)
+    segment = _pass_task(own_spec[None])
     squares_part, products_part = pair_stats(own_spec, segment, lag_table, angular)
     partner_ids = jnp.arange(segment.shape[0], dtype=jnp.int32)
     keep_mask = (partner_ids > block_rank).astype(jnp.float32)[:, None]

time: 172 us -> 160 us (0.930)
  blocking collectives: 73.1 us -> 41.8 us
  waiting for transfers between devices: 8.06 us -> 22.2 us
  starting transfers between devices: 7.28 us -> 10.9 us
    all_gather x1 -> x0, blocking collectives: 31.6 us -> none  [per_device(): segment = lax.all_gather(own_spec[None], 'pair', axis=0, tiled=True)]
    all_to_all x0 -> x1, waiting for transfers between devices: none -> 14 us  [_pass_task(): all_to_all(jnp.tile(s0, lanes), 'pair', split_axis=0, concat_axis=0, tile...]
    all_to_all x0 -> x1, starting transfers between devices: none -> 3.59 us  [_pass_task(): all_to_all(jnp.tile(s0, lanes), 'pair', split_axis=0, concat_axis=0, tile...]
  transfers between devices with their start and end apart: 1 -> 2, of which waited for: 1 -> 2; matrix products, arithmetic and copies ran while one was open for 0% -> 1% of each run, Pallas kernels for 0% -> 0%
where the time goes in v1:
time: 160 us; the launch traced here: 159 us
  other arithmetic  60.2 us (38%)
  blocking collectives  41.8 us (26%)
  waiting for transfers between devices  22.2 us (14%)
  starting transfers between devices  10.9 us (7%)
  local copies, waits for them, and re-layouts  10.1 us (6%)
  matrix products  6.83 us (4%)
  loops' own time  5.79 us (4%)
    psum x1, blocking collectives, per_device(): hessian, gradient = lax.psum((hessian, gradient), 'pair')  35.5 us
    cos x8, other arithmetic, band_table(): return jnp.concatenate([jnp.cos(angles), jnp.sin(angles)], axis=1)  33.2 us
    another operation x4, other arithmetic, per_device(): factor = jnp.linalg.cholesky(system)  23.6 us
    all_to_all x1, waiting for transfers between devices, _pass_task(): all_to_all(jnp.tile(s0, lanes), 'pair', split_axis=0, concat_axis=0, tile...  14 us
    all_to_all x1, waiting for transfers between devices, per_device(): lax.all_to_all(records, 'pair', split_axis=2, concat_axis=1, tiled=True)  8.26 us
    all_to_all x1, starting transfers between devices, per_device(): lax.all_to_all(records, 'pair', split_axis=2, concat_axis=1, tiled=True)  7.28 us
    psum x1, blocking collectives, per_device(): trace_sum = lax.psum(jnp.sum(diagonal), 'row')  6.25 us
    another operation x1, loops' own time, per_device(): lax.scan(accumulate, jnp.zeros((channels, 2 * NF), jnp.float32), jnp.aran...  5.79 us
  transfers between devices with their start and end apart: 2, of which 2 were waited for; matrix products, arithmetic and copies ran while one was open for 1% of the time, Pallas kernels for 0%

profile of v1, /device:TPU:0, one launch (start us, length us, event | category | flops | bytes accessed | tf_op | source)
XLA Modules:
  0.0 159.3 jit_solution(7879578481115024471)
XLA Ops:
  0.0 1.7 %copy.36 = bf16[32,512,8]{1,0,2:T(8,128)(2,1)} copy(bf16[32,512,8]{1,2,0:T(8,128)(2,1)} %param.6) | data formatting | bytes 524288 | tf_op args[0]
  1.7 7.3 %all-to-all-start = ((bf16[32,512,8]{1,0,2:T(8,128)(2,1)}), bf16[32,512,8]{1,0,2:T(8,128)(2,1)S(1)}, u32[]{:S(2)}, u32[]{:S(2)}) async-start(bf16[32,512,8]{1,0,2:T(8,128)(2,1)} %copy.36), calls=%async_computation | async-start | bytes 524288 | tf_op jit(solution)/shard_map/all_to_all | solution.py:56
  9.0 0.7 dynamic_slice.20
  9.7 8.3 %all-to-all-done = bf16[32,512,8]{1,0,2:T(8,128)(2,1)S(1)} async-done(((bf16[32,512,8]{1,0,2:T(8,128)(2,1)}), bf16[32,512,8]{1,0,2:T(8,128)(2,1)S(1)}, u32[]{:S(2)}, u32[]{:S(2)}) %all-to-all-start) | async-done | bytes 262176 | tf_op jit(solution)/shard_map/all_to_all | solution.py:56
  18.0 48.9 %while.13 = (s32[]{:T(128)}, f32[32,1024]{1,0:T(8,128)S(1)}, s32[8]{0:T(128)S(1)}, bf16[32,4096]{1,0:T(8,128)(2,1)S(1)}, s32[]{:T(128)}, /*index=5*/s32[1]{0:T(128)}, s32[]{:T(128)}, s32[]{:T(128)}) while((s32[]{:T(128)}, f32[32,1024]{1,0:T(8,128)S(1)}, s32[8]{0:T(128)S(1)}, bf16[32,4096]{1,0:T(8,128)(2,1)S(1)}, s32[]{:T(128)}, ...), condition=%wide.region_1.2_spmd.clone, body=%wide.region_0.1_spmd.clone.sunk | while | flops 75596808 | bytes 6889645 | solution.py:77
  18.0 0.7 dynamic_slice.34
  19.4 4.1 %fusion.70 = (f32[512,512]{1,0:T(8,128)S(1)}, f32[512,512]{1,0:T(8,128)S(1)}) fusion(s32[512]{0:T(512)S(1)} %get-tuple-element.138, s32[512]{0:T(512)S(1)} %get-tuple-element.139), kind=kLoop, calls=%fused_computation.16.clone.1 | loop fusion | flops 3670016 | bytes 2101248 | tf_op jit(solution)/shard_map/while/body/eval_jaxpr/cos | solution.py:25
  23.5 0.3 fusion.71
  23.8 0.3 convolution_add_fusion.2
  24.1 0.7 dynamic_slice.34
  25.5 4.1 %fusion.70 = (f32[512,512]{1,0:T(8,128)S(1)}, f32[512,512]{1,0:T(8,128)S(1)}) fusion(s32[512]{0:T(512)S(1)} %get-tuple-element.138, s32[512]{0:T(512)S(1)} %get-tuple-element.139), kind=kLoop, calls=%fused_computation.16.clone.1 | loop fusion | flops 3670016 | bytes 2101248 | tf_op jit(solution)/shard_map/while/body/eval_jaxpr/cos | solution.py:25
  29.6 0.3 fusion.71
  30.2 0.7 dynamic_slice.34
  31.6 4.1 %fusion.70 = (f32[512,512]{1,0:T(8,128)S(1)}, f32[512,512]{1,0:T(8,128)S(1)}) fusion(s32[512]{0:T(512)S(1)} %get-tuple-element.138, s32[512]{0:T(512)S(1)} %get-tuple-element.139), kind=kLoop, calls=%fused_computation.16.clone.1 | loop fusion | flops 3670016 | bytes 2101248 | tf_op jit(solution)/shard_map/while/body/eval_jaxpr/cos | solution.py:25
  35.8 0.3 fusion.71
  36.1 0.3 convolution_add_fusion.2
  36.3 0.7 dynamic_slice.34
  37.7 4.1 %fusion.70 = (f32[512,512]{1,0:T(8,128)S(1)}, f32[512,512]{1,0:T(8,128)S(1)}) fusion(s32[512]{0:T(512)S(1)} %get-tuple-element.138, s32[512]{0:T(512)S(1)} %get-tuple-element.139), kind=kLoop, calls=%fused_computation.16.clone.1 | loop fusion | flops 3670016 | bytes 2101248 | tf_op jit(solution)/shard_map/while/body/eval_jaxpr/cos | solution.py:25
  41.9 0.3 fusion.71
  42.2 0.3 convolution_add_fusion.2
  42.5 0.7 dynamic_slice.34
  43.8 4.1 %fusion.70 = (f32[512,512]{1,0:T(8,128)S(1)}, f32[512,512]{1,0:T(8,128)S(1)}) fusion(s32[512]{0:T(512)S(1)} %get-tuple-element.138, s32[512]{0:T(512)S(1)} %get-tuple-element.139), kind=kLoop, calls=%fused_computation.16.clone.1 | loop fusion | flops 3670016 | bytes 2101248 | tf_op jit(solution)/shard_map/while/body/eval_jaxpr/cos | solution.py:25
  48.0 0.3 fusion.71
  48.3 0.3 convolution_add_fusion.2
  48.6 0.7 dynamic_slice.34
  50.0 4.1 %fusion.70 = (f32[512,512]{1,0:T(8,128)S(1)}, f32[512,512]{1,0:T(8,128)S(1)}) fusion(s32[512]{0:T(512)S(1)} %get-tuple-element.138, s32[512]{0:T(512)S(1)} %get-tuple-element.139), kind=kLoop, calls=%fused_computation.16.clone.1 | loop fusion | flops 3670016 | bytes 2101248 | tf_op jit(solution)/shard_map/while/body/eval_jaxpr/cos | solution.py:25
  54.1 0.3 fusion.71
  54.4 0.3 convolution_add_fusion.2
  54.7 0.7 dynamic_slice.34
  56.1 4.1 %fusion.70 = (f32[512,512]{1,0:T(8,128)S(1)}, f32[512,512]{1,0:T(8,128)S(1)}) fusion(s32[512]{0:T(512)S(1)} %get-tuple-element.138, s32[512]{0:T(512)S(1)} %get-tuple-element.139), kind=kLoop, calls=%fused_computation.16.clone.1 | loop fusion | flops 3670016 | bytes 2101248 | tf_op jit(solution)/shard_map/while/body/eval_jaxpr/cos | solution.py:25
  60.2 0.3 fusion.71
  60.8 0.7 dynamic_slice.34
  62.2 4.1 %fusion.70 = (f32[512,512]{1,0:T(8,128)S(1)}, f32[512,512]{1,0:T(8,128)S(1)}) fusion(s32[512]{0:T(512)S(1)} %get-tuple-element.138, s32[512]{0:T(512)S(1)} %get-tuple-element.139), kind=kLoop, calls=%fused_computation.16.clone.1 | loop fusion | flops 3670016 | bytes 2101248 | tf_op jit(solution)/shard_map/while/body/eval_jaxpr/cos | solution.py:25
  66.4 0.3 fusion.71
  66.6 0.3 convolution_add_fusion.2
  66.9 0.4 add_reduce_fusion
  67.4 0.6 compare_select_fusion
  68.1 0.8 tile.2
  69.0 3.6 %all-to-all-start.1 = ((bf16[8,32,2,512]{3,1,2,0:T(8,128)(2,1)}), bf16[8,32,2,512]{3,1,2,0:T(8,128)(2,1)S(1)}, u32[]{:S(2)}, u32[]{:S(2)}) async-start(bf16[8,32,2,512]{3,1,2,0:T(8,128)(2,1)} %tile.2), calls=%async_computation.1 | async-start | bytes 1048576 | tf_op jit(solution)/shard_map/all_to_all | solution.py:16
  72.7 14.0 %all-to-all-done.1 = bf16[8,32,2,512]{3,1,2,0:T(8,128)(2,1)S(1)} async-done(((bf16[8,32,2,512]{3,1,2,0:T(8,128)(2,1)}), bf16[8,32,2,512]{3,1,2,0:T(8,128)(2,1)S(1)}, u32[]{:S(2)}, u32[]{:S(2)}) %all-to-all-start.1) | async-done | bytes 524320 | tf_op jit(solution)/shard_map/all_to_all | solution.py:16
  86.9 2.3 %fusion.28 = f32[2,8,32,256]{3,2,1,0:T(8,128)S(1)} fusion(bf16[1,8,32,512]{3,2,1,0:T(8,128)(2,1)S(1)} %get-tuple-element.99, bf16[1,8,32,512]{3,2,1,0:T(8,128)(2,1)S(1)} %get-tuple-element.98, s32[256]{0:T(256)S(1)} %iota_add_fusion.3, s32[512]{0:T(512)S(1)} %iota_add_fusion.2, f32[512]{0:T(512)S(1)} %multiply_multiply_fusion), kind=kOutput, calls=%fused_computation.45 | convolution fusion | flops 136577024 | bytes 1053696 | tf_op jit(solution)/shard_map/dot_general | solution.py:46
  89.6 35.5 %all-reduce = (f32[32,8,8]{0,1,2:T(8,128)S(1)}, f32[32,8]{0,1:T(8,128)S(1)}) all-reduce(f32[32,8,8]{0,1,2:T(8,128)S(1)} %multiply_subtract_fusion, f32[32,8]{0,1:T(8,128)S(1)} %get-tuple-element.104), channel_id=1, replica_groups=mesh['pair'=8,'row'=4] {'pair'}, use_global_device_ids=true, to_apply=%region_5.6 | all-reduce | flops 2304 | bytes 18432 | tf_op jit(solution)/shard_map/psum | solution.py:113
  125.1 0.6 gather_fusion
  125.7 0.7 reduce_sum.57
  127.1 6.3 %psum.22 = f32[]{:T(128)} all-reduce(f32[]{:T(128)} %reduce_sum.57), channel_id=1, replica_groups=mesh['pair'=8,'row'=4] {'row'}, use_global_device_ids=true, to_apply=%region_7.8 | all-reduce | flops 1 | bytes 8 | tf_op jit(solution)/shard_map/psum | solution.py:115
  134.2 23.5 %custom-call.11 = f32[32,8,8]{2,1,0:T(8,128)S(1)} custom-call(f32[32,8,8]{2,1,0:T(8,128)S(1)} %broadcast_multiply_fusion), custom_call_target="Cholesky" | custom-call | tf_op jit(solution)/shard_map/jit(cholesky)/cholesky | solution.py:119
  158.1 0.7 custom-call.12
  158.8 0.5 dynamic-slice_bitcast_fusion
  (47 shorter events, 2.0 us)
Async XLA Ops:
  0.0 9.0 %copy-start.1 = (s32[8]{0:T(128)S(1)}, s32[8]{0:T(128)}, u32[]{:S(2)}) copy-start(s32[8]{0:T(128)} %param.8) | copy-start | bytes 100
  1.7 16.2 %all-to-all-start = ((bf16[32,512,8]{1,0,2:T(8,128)(2,1)}), bf16[32,512,8]{1,0,2:T(8,128)(2,1)S(1)}, u32[]{:S(2)}, u32[]{:S(2)}) async-start(bf16[32,512,8]{1,0,2:T(8,128)(2,1)} %copy.36), calls=%async_computation | async-start | bytes 524288 | tf_op jit(solution)/shard_map/all_to_all | solution.py:56
  18.0 49.0 %copy-start = (f32[1,32]{1,0:T(1,128)S(1)}, f32[1,32]{1,0:T(1,128)}, u32[]{:S(2)}) copy-start(f32[1,32]{1,0:T(1,128)} %param.7) | copy-start | bytes 388
  69.0 17.8 %all-to-all-start.1 = ((bf16[8,32,2,512]{3,1,2,0:T(8,128)(2,1)}), bf16[8,32,2,512]{3,1,2,0:T(8,128)(2,1)S(1)}, u32[]{:S(2)}, u32[]{:S(2)}) async-start(bf16[8,32,2,512]{3,1,2,0:T(8,128)(2,1)} %tile.2), calls=%async_computation.1 | async-start | bytes 1048576 | tf_op jit(solution)/shard_map/all_to_all | solution.py:16
